TPU v7x, 128 devices: a whole 4x4x4 slice. The times are simulated.
128 devices in a mesh: seq: 16 (over y, z_lo, core), vis: 8 (over z_hi, x).
Axes of the slice: x: 4, y: 4, z: 4 (z_hi: 2, z_lo: 2; z = z_hi * 2 + z_lo), core: 2. Of those that a mesh axis runs over, the one named last changes fastest.
Arguments:
- text: bfloat16 [4096, 8192], P('seq'), may hold values from -6 to 6
- frames: bfloat16 [4096, 8192], P(('seq', 'vis')), may hold values from -60 to 60
- tile_pos: int32 [4096], P(('seq', 'vis')), may hold values from 0 to 4095, as said below
- frame_count: int32 [128], P(('seq', 'vis')), may hold values from 2 to 32
- doc_ids: int32 [4096], replicated, may hold values from 0 to 3, never falling along the last dimension, each value on 1 to 2048 neighbouring positions
- norm_gain: float32 [8192], replicated, may hold values from 0.1 to 1.9
- w_query: bfloat16 [8192, 8192], P(None, 'vis'), may hold values from -4 to 4
- q_bias: float32 [8192], P('vis'), may hold values from -3 to 3
- w_key: bfloat16 [8192, 1024], P(None, 'vis'), may hold values from -4 to 4
- w_value: bfloat16 [8192, 1024], P(None, 'vis'), may hold values from -0.0625 to 0.0625
- v_bias: float32 [1024], P('vis'), may hold values from -3 to 3
Outputs:
- attended: bfloat16 [4096, 8192], P('seq', 'vis')
Inputs may be any that keep to these rules, and one draw needn't show every extreme that they name: `tile_pos`: all entries together name every position of the window once. Of one device's 32 rows, at most 2 of those below its frame_count fall into one shard of 256 positions, and in every draw one shard receives exactly 2 usable rows from every device. Rows at or beyond the count are unused. `doc_ids`: never falling along the window.
All inputs are finite; a program needn't handle non-finite values.
Results may differ from a plain program's by a relative error of at most 0.0069.
Values may be sent and summed in bfloat16 or wider, within the bound.
A program may use at most 128 MiB of HBM per device.

v0:
```python
import jax
import jax.numpy as jnp
from jax import lax
from jax.sharding import PartitionSpec as P

HEAD_DIM = 128
epsilon = 1e-06
negative = -1e30


def frame_slots(frames, tile_pos, frame_count, shard_rows, owners, capacity):
    row_count = frames.shape[0]
    row_ids = jnp.arange(row_count, dtype=jnp.int32)
    usable = row_ids < frame_count[0]
    owner = jnp.where(usable, tile_pos // shard_rows, owners)
    hits = (owner[:, None] == jnp.arange(owners, dtype=jnp.int32)[None, :]).astype(jnp.int32)
    earlier = (row_ids[:, None] > row_ids[None, :]).astype(jnp.int32)
    before = jnp.dot(earlier, hits, preferred_element_type=jnp.int32)
    rank = jnp.sum(before * hits, axis=1)
    slot_index = owner * capacity + rank
    slot_ids = jnp.arange(owners * capacity, dtype=jnp.int32)
    match = usable[:, None] & (slot_index[:, None] == slot_ids[None, :])
    filled = jnp.any(match, axis=0)
    source = jnp.sum(jnp.where(match, row_ids[:, None], 0), axis=0)
    slot_rows = jnp.where(filled[:, None], frames[source], jnp.zeros((), frames.dtype))
    slot_place = jnp.where(filled, tile_pos[source], -1)
    return (
        slot_rows.reshape(owners, capacity, frames.shape[1]),
        slot_place.reshape(owners, capacity),
    )


def place_frames(text, incoming, incoming_place, first_row):
    local_place = incoming_place - first_row
    lookup = local_place[None, :] == jnp.arange(text.shape[0], dtype=jnp.int32)[:, None]
    covered = jnp.any(lookup, axis=1)
    source = jnp.sum(
        jnp.where(lookup, jnp.arange(local_place.shape[0], dtype=jnp.int32)[None, :], 0), axis=1
    )
    return jnp.where(covered[:, None], incoming[source], text)


def attend_block(
    block_state, query_rows, query_place, query_docs, key_block, key_place, key_docs, kv_heads
):
    row_peak, row_total, summed = block_state
    row_count = query_rows.shape[0]
    grouped = query_rows.reshape(row_count, kv_heads, -1, HEAD_DIM)
    key_width = kv_heads * HEAD_DIM
    key_part = key_block[:, :key_width].reshape(-1, kv_heads, HEAD_DIM)
    value_part = key_block[:, key_width:].reshape(-1, kv_heads, HEAD_DIM)
    scores = jnp.einsum(
        "qgjd,kgd->qgjk", grouped, key_part, preferred_element_type=jnp.float32
    ) * HEAD_DIM ** (-0.5)
    allowed = (key_place[None, :] <= query_place[:, None]) & (
        key_docs[None, :] == query_docs[:, None]
    )
    allowed = allowed[:, None, None, :]
    block_peak = jnp.max(jnp.where(allowed, scores, negative), axis=3)
    new_peak = jnp.maximum(row_peak, block_peak)
    raised = jnp.where(allowed, jnp.exp(scores - new_peak[..., None]), 0.0)
    factor = jnp.exp(row_peak - new_peak)
    new_total = row_total * factor + jnp.sum(raised, axis=3)
    product = jnp.einsum(
        "qgjk,kgd->qgjd",
        raised.astype(jnp.bfloat16),
        value_part,
        preferred_element_type=jnp.float32,
    )
    return (new_peak, new_total, summed * factor[..., None] + product)


def on_device(
    text, frames, tile_pos, frame_count, doc_ids, norm_gain, w_query, q_bias, w_key, w_value, v_bias
):
    seq_count = lax.axis_size("seq")
    vis_count = lax.axis_size("vis")
    shard_index = lax.axis_index("seq")
    shard_rows = text.shape[0]
    capacity = shard_rows // (seq_count * vis_count)
    first_row = shard_index * shard_rows
    slot_rows, slot_place = frame_slots(
        frames, tile_pos, frame_count, shard_rows, seq_count, capacity
    )
    wide_rows = jnp.broadcast_to(slot_rows[:, None], (seq_count, vis_count) + slot_rows.shape[1:])
    wide_rows = wide_rows.reshape(seq_count * vis_count, capacity, slot_rows.shape[2])
    wide_place = jnp.broadcast_to(slot_place[:, None], (seq_count, vis_count, capacity))
    wide_place = wide_place.reshape(seq_count * vis_count, capacity)
    incoming, incoming_place = (
        lax.all_to_all(wide_rows, ("seq", "vis"), split_axis=0, concat_axis=0, tiled=True),
        lax.all_to_all(wide_place, ("seq", "vis"), split_axis=0, concat_axis=0, tiled=True),
    )
    incoming = incoming.reshape(-1, incoming.shape[-1])
    incoming_place = incoming_place.reshape(-1)
    merged = place_frames(text, incoming, incoming_place, first_row)
    widened = merged.astype(jnp.float32)
    mean_square = jnp.mean(widened * widened, axis=1, keepdims=True)
    normed = (widened * lax.rsqrt(mean_square + epsilon) * norm_gain).astype(jnp.bfloat16)
    queries = (jnp.dot(normed, w_query, preferred_element_type=jnp.float32) + q_bias).astype(
        jnp.bfloat16
    )
    key_rows = jnp.dot(normed, w_key, preferred_element_type=jnp.float32).astype(jnp.bfloat16)
    value_rows = (jnp.dot(normed, w_value, preferred_element_type=jnp.float32) + v_bias).astype(
        jnp.bfloat16
    )
    keyval = jnp.concatenate([key_rows, value_rows], axis=1)
    kv_heads = w_key.shape[1] // HEAD_DIM
    per_group = w_query.shape[1] // HEAD_DIM // kv_heads
    own_place = first_row + jnp.arange(shard_rows, dtype=jnp.int32)
    own_docs = lax.dynamic_slice_in_dim(doc_ids, first_row, shard_rows)
    blocks = [(queries, own_place, own_docs)]
    initial = tuple(
        (
            (
                jnp.full((entry[0].shape[0], kv_heads, per_group), negative, jnp.float32),
                jnp.zeros((entry[0].shape[0], kv_heads, per_group), jnp.float32),
                jnp.zeros((entry[0].shape[0], kv_heads, per_group, HEAD_DIM), jnp.float32),
            )
            for entry in blocks
        )
    )
    incoming_keys = lax.all_gather(keyval, "seq", axis=0, tiled=True)
    piece_rows = incoming_keys.shape[0]
    step_rows = 512

    def one_step(step_index, current):
        key_first = step_index * step_rows
        key_block = lax.dynamic_slice_in_dim(incoming_keys, step_index * step_rows, step_rows)
        key_place = key_first + jnp.arange(step_rows, dtype=jnp.int32)
        key_docs = lax.dynamic_slice_in_dim(doc_ids, key_first, step_rows)
        updated = []
        for entry, block_state in zip(blocks, current):
            query_rows, query_place, query_docs = entry

            def compute(
                operand, query_rows=query_rows, query_place=query_place, query_docs=query_docs
            ):
                return attend_block(
                    operand,
                    query_rows,
                    query_place,
                    query_docs,
                    key_block,
                    key_place,
                    key_docs,
                    kv_heads,
                )

            def unchanged(operand):
                return operand

            updated.append(lax.cond(key_first <= query_place[-1], compute, unchanged, block_state))
        return tuple(updated)

    finals = lax.fori_loop(0, piece_rows // step_rows, one_step, initial)
    outputs = [
        (summed / row_total[..., None]).reshape(summed.shape[0], -1).astype(jnp.bfloat16)
        for row_peak, row_total, summed in finals
    ]
    return outputs[0]


def solution(mesh):
    in_specs = (
        P("seq", None),
        P(("seq", "vis"), None),
        P(("seq", "vis")),
        P(("seq", "vis")),
        P(),
        P(),
        P(None, "vis"),
        P("vis"),
        P(None, "vis"),
        P(None, "vis"),
        P("vis"),
    )
    out_specs = P("seq", "vis")
    return jax.shard_map(
        on_device, mesh=mesh, in_specs=in_specs, out_specs=out_specs, check_vma=False
    )
```

profile of v0, /device:TPU:57, one launch (start us, length us, event | category | flops | bytes accessed | tf_op | source)
XLA Modules:
  0.0 259.8 jit_solution(562289550122915700)
XLA Ops:
  11.2 10.4 %all-to-all-start = ((s32[128,1,2]{2,1,0:T(1,128)}), s32[128,1,2]{2,1,0:T(1,128)S(1)}, u32[]{:S(2)}, u32[]{:S(2)}) async-start(s32[128,1,2]{2,1,0:T(1,128)} %bitcast.16), calls=%async_computation | async-start | bytes 131072 | tf_op jit(solution)/shard_map/all_to_all | solution.py:91
  28.7 6.1 %broadcast_in_dim.133 = bf16[16,8,2,8192]{3,2,1,0:T(2,128)(2,1)} broadcast(bf16[16,2,8192]{2,1,0:T(2,128)(2,1)S(1)} %broadcast_select_fusion.1), dimensions={0,2,3} | broadcast | bytes 4718592 | tf_op jit(solution)/shard_map/broadcast_in_dim | solution.py:85
  34.8 8.2 %all-to-all-start.1 = ((bf16[128,2,8192]{2,1,0:T(2,128)(2,1)}), bf16[128,2,8192]{2,1,0:T(2,128)(2,1)}, u32[]{:S(2)}, u32[]{:S(2)}) async-start(bf16[128,2,8192]{2,1,0:T(2,128)(2,1)} %bitcast.83), calls=%async_computation.1 | async-start | bytes 8388608 | tf_op jit(solution)/shard_map/all_to_all | solution.py:90
  43.6 48.8 %all-to-all-done.1 = bf16[128,2,8192]{2,1,0:T(2,128)(2,1)} async-done(((bf16[128,2,8192]{2,1,0:T(2,128)(2,1)}), bf16[128,2,8192]{2,1,0:T(2,128)(2,1)}, u32[]{:S(2)}, u32[]{:S(2)}) %all-to-all-start.1) | async-done | bytes 4194336 | tf_op jit(solution)/shard_map/all_to_all | solution.py:90
  92.5 7.2 %reshape.191 = bf16[256,8192]{1,0:T(8,128)(2,1)} reshape(bf16[128,2,8192]{2,1,0:T(2,128)(2,1)} %all-to-all-done.1) | data formatting | bytes 8388608 | tf_op jit(solution)/shard_map/reshape | solution.py:93
  99.7 11.7 %gather_fusion.2 = bf16[256,8192]{1,0:T(8,128)(2,1)} fusion(bf16[256,8192]{1,0:T(8,128)(2,1)} %reshape.191, s32[1024]{0:T(1024)S(1)} %pad_clamp_fusion), kind=kCustom, calls=%fused_computation.2 | custom fusion | bytes 8389632 | tf_op jit(solution)/shard_map/gather | solution.py:40
  111.3 5.1 %fusion.22 = f32[256]{0:T(256)S(1)} fusion(bf16[256,8192]{1,0:T(8,128)(2,1)} %gather_fusion.2, bf16[256,8192]{1,0:T(8,128)(2,1)} %param.15, pred[256]{0:T(512)(128)(4,1)S(1)} %fusion.28), kind=kLoop, calls=%fused_computation.31 | loop fusion | flops 8388352 | bytes 8389888 | tf_op jit(solution)/shard_map/reduce_sum | solution.py:97
  126.2 12.3 %fusion.25 = bf16[256,1024]{1,0:T(8,128)(2,1)} fusion(bf16[256,8192]{1,0:T(8,128)(2,1)} %copy-done.2, bf16[8192,1024]{1,0:T(8,128)(2,1)} %param.21, f32[1024]{0:T(1024)S(1)} %copy-done.8), kind=kOutput, calls=%fused_computation.36 | convolution fusion | flops 4295491584 | bytes 21499904 | tf_op jit(solution)/shard_map/dot_general | solution.py:99
  138.5 22.6 %all-gather.2.cloned.1.call-done = bf16[4096,256]{0,1:T(8,128)(2,1)} async-done(((bf16[256,256]{0,1:T(8,128)(2,1)}), bf16[4096,256]{0,1:T(8,128)(2,1)}) %all-gather.2.cloned.1.call-update) | async-done | bytes 2097168 | tf_op jit(solution)/shard_map/all_gather | solution.py:122
  161.1 4.1 %copy.30 = bf16[4096,256]{1,0:T(8,128)(2,1)} copy(bf16[4096,256]{0,1:T(8,128)(2,1)} %all-gather.2.cloned.1.call-done) | data formatting | bytes 4194304 | tf_op jit(solution)/shard_map/while | solution.py:155
  165.3 84.8 %while.17 = (s32[]{:T(128)}, f32[256,1,8]{0,2,1:T(8,128)S(1)}, f32[256,1,8]{0,2,1:T(8,128)S(1)}, f32[256,1,8,128]{0,3,2,1:T(8,128)S(1)}, s32[256]{0:T(256)S(1)},...) while((s32[]{:T(128)}, f32[256,1,8]{0,2,1:T(8,128)S(1)}, ...), condition=%wide.region_11.12_spmd, body=%wide.region_6.11_spmd.sunk | while | flops 549329408 | bytes 32915828 | solution.py:155
  166.6 9.3 %conditional.2 = ((f32[256,1,8]{0,2,1:T(8,128)S(1)}, f32[256,1,8]{0,2,1:T(8,128)S(1)}, f32[256,1,8,128]{0,3,2,1:T(8,128)S(1)})) conditional(s32[]{:T(128)} %convert_element_type.65, (f32[256,1,8]{0,2,1:T(8,128)S(1)}, f32[256,1,8]{0,2,1:T(8,128)S(1)}, f32[256,1,8,128]{0,3,2,1:T(8,128)S(1)}) %tuple.52, (s32[]{:T(128)}, s32[512]{0:T(512)S(1)}, ...), branch_computations={%region_7.7_spmd, %region_8.10_spmd} | conditional | flops 549329408 | bytes 32913534 | solution.py:152
  167.6 3.8 %fusion = (f32[256,8]{0,1:T(8,128)S(1)}, f32[512,256,8]{1,0,2:T(8,128)}) fusion(pred[256,512]{0,1:T(8,128)(4,1)S(1)} %compare_and_fusion, bf16[4096,256]{1,0:T(8,128)(2,1)} %get-tuple-element.272, s32[]{:T(128)S(6)} %select_n.70, bf16[256,1024]{1,0:T(8,128)(2,1)} %get-tuple-element.273), kind=kOutput, calls=%fused_computation.5 | convolution fusion | flops 271579136 | bytes 4988932 | tf_op jit(solution)/shard_map/while/body/eval_jaxpr/cond/branch_1_fun/qgjd,kgd->qgjk/dot_general | solution.py:52
  177.2 9.3 %conditional.2 = ((f32[256,1,8]{0,2,1:T(8,128)S(1)}, f32[256,1,8]{0,2,1:T(8,128)S(1)}, f32[256,1,8,128]{0,3,2,1:T(8,128)S(1)})) conditional(s32[]{:T(128)} %convert_element_type.65, (f32[256,1,8]{0,2,1:T(8,128)S(1)}, f32[256,1,8]{0,2,1:T(8,128)S(1)}, f32[256,1,8,128]{0,3,2,1:T(8,128)S(1)}) %tuple.52, (s32[]{:T(128)}, s32[512]{0:T(512)S(1)}, ...), branch_computations={%region_7.7_spmd, %region_8.10_spmd} | conditional | flops 549329408 | bytes 32913534 | solution.py:152
  178.2 3.8 %fusion = (f32[256,8]{0,1:T(8,128)S(1)}, f32[512,256,8]{1,0,2:T(8,128)}) fusion(pred[256,512]{0,1:T(8,128)(4,1)S(1)} %compare_and_fusion, bf16[4096,256]{1,0:T(8,128)(2,1)} %get-tuple-element.272, s32[]{:T(128)S(6)} %select_n.70, bf16[256,1024]{1,0:T(8,128)(2,1)} %get-tuple-element.273), kind=kOutput, calls=%fused_computation.5 | convolution fusion | flops 271579136 | bytes 4988932 | tf_op jit(solution)/shard_map/while/body/eval_jaxpr/cond/branch_1_fun/qgjd,kgd->qgjk/dot_general | solution.py:52
  187.7 9.3 %conditional.2 = ((f32[256,1,8]{0,2,1:T(8,128)S(1)}, f32[256,1,8]{0,2,1:T(8,128)S(1)}, f32[256,1,8,128]{0,3,2,1:T(8,128)S(1)})) conditional(s32[]{:T(128)} %convert_element_type.65, (f32[256,1,8]{0,2,1:T(8,128)S(1)}, f32[256,1,8]{0,2,1:T(8,128)S(1)}, f32[256,1,8,128]{0,3,2,1:T(8,128)S(1)}) %tuple.52, (s32[]{:T(128)}, s32[512]{0:T(512)S(1)}, ...), branch_computations={%region_7.7_spmd, %region_8.10_spmd} | conditional | flops 549329408 | bytes 32913534 | solution.py:152
  188.8 3.8 %fusion = (f32[256,8]{0,1:T(8,128)S(1)}, f32[512,256,8]{1,0,2:T(8,128)}) fusion(pred[256,512]{0,1:T(8,128)(4,1)S(1)} %compare_and_fusion, bf16[4096,256]{1,0:T(8,128)(2,1)} %get-tuple-element.272, s32[]{:T(128)S(6)} %select_n.70, bf16[256,1024]{1,0:T(8,128)(2,1)} %get-tuple-element.273), kind=kOutput, calls=%fused_computation.5 | convolution fusion | flops 271579136 | bytes 4988932 | tf_op jit(solution)/shard_map/while/body/eval_jaxpr/cond/branch_1_fun/qgjd,kgd->qgjk/dot_general | solution.py:52
  198.3 9.3 %conditional.2 = ((f32[256,1,8]{0,2,1:T(8,128)S(1)}, f32[256,1,8]{0,2,1:T(8,128)S(1)}, f32[256,1,8,128]{0,3,2,1:T(8,128)S(1)})) conditional(s32[]{:T(128)} %convert_element_type.65, (f32[256,1,8]{0,2,1:T(8,128)S(1)}, f32[256,1,8]{0,2,1:T(8,128)S(1)}, f32[256,1,8,128]{0,3,2,1:T(8,128)S(1)}) %tuple.52, (s32[]{:T(128)}, s32[512]{0:T(512)S(1)}, ...), branch_computations={%region_7.7_spmd, %region_8.10_spmd} | conditional | flops 549329408 | bytes 32913534 | solution.py:152
  199.3 3.8 %fusion = (f32[256,8]{0,1:T(8,128)S(1)}, f32[512,256,8]{1,0,2:T(8,128)}) fusion(pred[256,512]{0,1:T(8,128)(4,1)S(1)} %compare_and_fusion, bf16[4096,256]{1,0:T(8,128)(2,1)} %get-tuple-element.272, s32[]{:T(128)S(6)} %select_n.70, bf16[256,1024]{1,0:T(8,128)(2,1)} %get-tuple-element.273), kind=kOutput, calls=%fused_computation.5 | convolution fusion | flops 271579136 | bytes 4988932 | tf_op jit(solution)/shard_map/while/body/eval_jaxpr/cond/branch_1_fun/qgjd,kgd->qgjk/dot_general | solution.py:52
  208.9 9.3 %conditional.2 = ((f32[256,1,8]{0,2,1:T(8,128)S(1)}, f32[256,1,8]{0,2,1:T(8,128)S(1)}, f32[256,1,8,128]{0,3,2,1:T(8,128)S(1)})) conditional(s32[]{:T(128)} %convert_element_type.65, (f32[256,1,8]{0,2,1:T(8,128)S(1)}, f32[256,1,8]{0,2,1:T(8,128)S(1)}, f32[256,1,8,128]{0,3,2,1:T(8,128)S(1)}) %tuple.52, (s32[]{:T(128)}, s32[512]{0:T(512)S(1)}, ...), branch_computations={%region_7.7_spmd, %region_8.10_spmd} | conditional | flops 549329408 | bytes 32913534 | solution.py:152
  209.9 3.8 %fusion = (f32[256,8]{0,1:T(8,128)S(1)}, f32[512,256,8]{1,0,2:T(8,128)}) fusion(pred[256,512]{0,1:T(8,128)(4,1)S(1)} %compare_and_fusion, bf16[4096,256]{1,0:T(8,128)(2,1)} %get-tuple-element.272, s32[]{:T(128)S(6)} %select_n.70, bf16[256,1024]{1,0:T(8,128)(2,1)} %get-tuple-element.273), kind=kOutput, calls=%fused_computation.5 | convolution fusion | flops 271579136 | bytes 4988932 | tf_op jit(solution)/shard_map/while/body/eval_jaxpr/cond/branch_1_fun/qgjd,kgd->qgjk/dot_general | solution.py:52
  219.5 9.3 %conditional.2 = ((f32[256,1,8]{0,2,1:T(8,128)S(1)}, f32[256,1,8]{0,2,1:T(8,128)S(1)}, f32[256,1,8,128]{0,3,2,1:T(8,128)S(1)})) conditional(s32[]{:T(128)} %convert_element_type.65, (f32[256,1,8]{0,2,1:T(8,128)S(1)}, f32[256,1,8]{0,2,1:T(8,128)S(1)}, f32[256,1,8,128]{0,3,2,1:T(8,128)S(1)}) %tuple.52, (s32[]{:T(128)}, s32[512]{0:T(512)S(1)}, ...), branch_computations={%region_7.7_spmd, %region_8.10_spmd} | conditional | flops 549329408 | bytes 32913534 | solution.py:152
  230.1 9.3 %conditional.2 = ((f32[256,1,8]{0,2,1:T(8,128)S(1)}, f32[256,1,8]{0,2,1:T(8,128)S(1)}, f32[256,1,8,128]{0,3,2,1:T(8,128)S(1)})) conditional(s32[]{:T(128)} %convert_element_type.65, (f32[256,1,8]{0,2,1:T(8,128)S(1)}, f32[256,1,8]{0,2,1:T(8,128)S(1)}, f32[256,1,8,128]{0,3,2,1:T(8,128)S(1)}) %tuple.52, (s32[]{:T(128)}, s32[512]{0:T(512)S(1)}, ...), branch_computations={%region_7.7_spmd, %region_8.10_spmd} | conditional | flops 549329408 | bytes 32913534 | solution.py:152
  240.7 9.3 %conditional.2 = ((f32[256,1,8]{0,2,1:T(8,128)S(1)}, f32[256,1,8]{0,2,1:T(8,128)S(1)}, f32[256,1,8,128]{0,3,2,1:T(8,128)S(1)})) conditional(s32[]{:T(128)} %convert_element_type.65, (f32[256,1,8]{0,2,1:T(8,128)S(1)}, f32[256,1,8]{0,2,1:T(8,128)S(1)}, f32[256,1,8,128]{0,3,2,1:T(8,128)S(1)}) %tuple.52, (s32[]{:T(128)}, s32[512]{0:T(512)S(1)}, ...), branch_computations={%region_7.7_spmd, %region_8.10_spmd} | conditional | flops 549329408 | bytes 32913534 | solution.py:152
  (152 shorter events, 83.8 us)
Async XLA Ops:
  6.5 113.5 %copy-start = (bf16[8192,128]{1,0:T(8,128)(2,1)S(1)}, bf16[8192,128]{1,0:T(8,128)(2,1)}, u32[]{:S(2)}) copy-start(bf16[8192,128]{1,0:T(8,128)(2,1)} %param.23) | copy-start | bytes 6291460
  11.2 17.4 %all-to-all-start = ((s32[128,1,2]{2,1,0:T(1,128)}), s32[128,1,2]{2,1,0:T(1,128)S(1)}, u32[]{:S(2)}, u32[]{:S(2)}) async-start(s32[128,1,2]{2,1,0:T(1,128)} %bitcast.16), calls=%async_computation | async-start | bytes 131072 | tf_op jit(solution)/shard_map/all_to_all | solution.py:91
  34.8 57.7 %all-to-all-start.1 = ((bf16[128,2,8192]{2,1,0:T(2,128)(2,1)}), bf16[128,2,8192]{2,1,0:T(2,128)(2,1)}, u32[]{:S(2)}, u32[]{:S(2)}) async-start(bf16[128,2,8192]{2,1,0:T(2,128)(2,1)} %bitcast.83), calls=%async_computation.1 | async-start | bytes 8388608 | tf_op jit(solution)/shard_map/all_to_all | solution.py:90
  43.0 118.1 %all-gather.2.cloned.1.call-start = ((), (), s32[]{:S(2)}) async-start(), calls=%async_computation.2 | async-start | bytes 2228224 | tf_op jit(solution)/shard_map/all_gather | solution.py:122
  99.7 16.8 %copy-start.6 = (f32[8192]{0:T(1024)S(1)}, f32[8192]{0:T(1024)}, u32[]{:S(2)}) copy-start(f32[8192]{0:T(1024)} %param.20) | copy-start | bytes 98308
  111.3 5.2 %copy-start.3 = (bf16[256,8192]{1,0:T(8,128)(2,1)S(1)}, bf16[256,8192]{1,0:T(8,128)(2,1)}, u32[]{:S(2)}) copy-start(bf16[256,8192]{1,0:T(8,128)(2,1)} %gather_fusion.2) | copy-start | bytes 12582916
  111.3 5.9 %copy-start.4 = (bf16[256,8192]{1,0:T(8,128)(2,1)S(1)}, bf16[256,8192]{1,0:T(8,128)(2,1)}, u32[]{:S(2)}) copy-start(bf16[256,8192]{1,0:T(8,128)(2,1)} %param.15) | copy-start | bytes 12582916
  120.1 4.7 %copy-start.2 = (bf16[256,8192]{1,0:T(8,128)(2,1)}, bf16[256,8192]{1,0:T(8,128)(2,1)S(1)}, u32[]{:S(2)}) copy-start(bf16[256,8192]{1,0:T(8,128)(2,1)S(1)} %fusion.24) | copy-start | bytes 12582916
  120.1 3.1 %copy-start.5 = (bf16[8192,128]{1,0:T(8,128)(2,1)S(1)}, bf16[8192,128]{1,0:T(8,128)(2,1)}, u32[]{:S(2)}) copy-start(bf16[8192,128]{1,0:T(8,128)(2,1)} %param.24) | copy-start | bytes 6291460
  120.1 3.1 %copy-start.7 = (f32[128]{0:T(128)S(1)}, f32[128]{0:T(128)}, u32[]{:S(2)}) copy-start(f32[128]{0:T(128)} %param.25) | copy-start | bytes 1540
  123.2 3.0 %copy-start.8 = (f32[1024]{0:T(1024)S(1)}, f32[1024]{0:T(1024)}, u32[]{:S(2)}) copy-start(f32[1024]{0:T(1024)} %param.22) | copy-start | bytes 12292
  171.4 3.6 %copy-start.1 = (f32[512,256,8]{1,0,2:T(8,128)S(1)}, f32[512,256,8]{1,0,2:T(8,128)}, u32[]{:S(2)}) copy-start(f32[512,256,8]{1,0,2:T(8,128)} %get-tuple-element.350) | copy-start | bytes 12582916 | tf_op jit(solution)/shard_map/while/body/eval_jaxpr/cond
  182.0 3.6 %copy-start.1 = (f32[512,256,8]{1,0,2:T(8,128)S(1)}, f32[512,256,8]{1,0,2:T(8,128)}, u32[]{:S(2)}) copy-start(f32[512,256,8]{1,0,2:T(8,128)} %get-tuple-element.350) | copy-start | bytes 12582916 | tf_op jit(solution)/shard_map/while/body/eval_jaxpr/cond
  192.6 3.6 %copy-start.1 = (f32[512,256,8]{1,0,2:T(8,128)S(1)}, f32[512,256,8]{1,0,2:T(8,128)}, u32[]{:S(2)}) copy-start(f32[512,256,8]{1,0,2:T(8,128)} %get-tuple-element.350) | copy-start | bytes 12582916 | tf_op jit(solution)/shard_map/while/body/eval_jaxpr/cond
  203.2 3.6 %copy-start.1 = (f32[512,256,8]{1,0,2:T(8,128)S(1)}, f32[512,256,8]{1,0,2:T(8,128)}, u32[]{:S(2)}) copy-start(f32[512,256,8]{1,0,2:T(8,128)} %get-tuple-element.350) | copy-start | bytes 12582916 | tf_op jit(solution)/shard_map/while/body/eval_jaxpr/cond
  213.8 3.6 %copy-start.1 = (f32[512,256,8]{1,0,2:T(8,128)S(1)}, f32[512,256,8]{1,0,2:T(8,128)}, u32[]{:S(2)}) copy-start(f32[512,256,8]{1,0,2:T(8,128)} %get-tuple-element.350) | copy-start | bytes 12582916 | tf_op jit(solution)/shard_map/while/body/eval_jaxpr/cond
  224.4 3.6 %copy-start.1 = (f32[512,256,8]{1,0,2:T(8,128)S(1)}, f32[512,256,8]{1,0,2:T(8,128)}, u32[]{:S(2)}) copy-start(f32[512,256,8]{1,0,2:T(8,128)} %get-tuple-element.350) | copy-start | bytes 12582916 | tf_op jit(solution)/shard_map/while/body/eval_jaxpr/cond
  235.0 3.6 %copy-start.1 = (f32[512,256,8]{1,0,2:T(8,128)S(1)}, f32[512,256,8]{1,0,2:T(8,128)}, u32[]{:S(2)}) copy-start(f32[512,256,8]{1,0,2:T(8,128)} %get-tuple-element.350) | copy-start | bytes 12582916 | tf_op jit(solution)/shard_map/while/body/eval_jaxpr/cond
  245.5 3.6 %copy-start.1 = (f32[512,256,8]{1,0,2:T(8,128)S(1)}, f32[512,256,8]{1,0,2:T(8,128)}, u32[]{:S(2)}) copy-start(f32[512,256,8]{1,0,2:T(8,128)} %get-tuple-element.350) | copy-start | bytes 12582916 | tf_op jit(solution)/shard_map/while/body/eval_jaxpr/cond
Sparse Core Ops, SparseCore 0:
  125.5 35.5 all-gather.1
where the time goes:
time: 261 us; the launch traced here: 260 us
  waiting for transfers between devices  75.1 us (29%)
  matrix products  74.8 us (29%)
  local copies, waits for them, and re-layouts  50.3 us (19%)
  other arithmetic  20.7 us (8%)
  starting transfers between devices  18.6 us (7%)
  between operations  14.4 us (6%)
  loops' own time  5.92 us (2%)
    all_to_all x1, waiting for transfers between devices, on_device(): lax.all_to_all(wide_rows, ('seq', 'vis'), split_axis=0, concat_axis=0, ti...  48.8 us
    dot_general x8, matrix products, attend_block(): jnp.einsum('qgjd,kgd->qgjk', grouped, key_part, preferred_element_type=jn...  30.6 us
    dot_general x8, matrix products, attend_block(): jnp.einsum('qgjk,kgd->qgjd', raised.astype(jnp.bfloat16), value_part, pre...  28.5 us
    all_gather x1, waiting for transfers between devices, on_device(): incoming_keys = lax.all_gather(keyval, 'seq', axis=0, tiled=True)  22.6 us
    dot_general x1, matrix products, on_device(): jnp.dot(normed, w_query, preferred_element_type=jnp.float32) + q_bias  12.3 us
    gather x1, local copies, waits for them, and re-layouts, place_frames(): return jnp.where(covered[:, None], incoming[source], text)  11.7 us
    all_to_all x1, starting transfers between devices, on_device(): lax.all_to_all(wide_place, ('seq', 'vis'), split_axis=0, concat_axis=0, t...  10.4 us
    all_to_all x1, starting transfers between devices, on_device(): lax.all_to_all(wide_rows, ('seq', 'vis'), split_axis=0, concat_axis=0, ti...  8.19 us
  transfers between devices with their start and end apart: 3, of which 3 were waited for; matrix products, arithmetic and copies ran while one was open for 7% of the time, Pallas kernels for 0%

commit v1 on v0

--- a/solution.py
+++ b/solution.py
@@ -119,7 +119,9 @@
             for entry in blocks
         )
     )
-    incoming_keys = lax.all_gather(keyval, "seq", axis=0, tiled=True)
+    incoming_keys = jnp.concatenate(
+        lax.all_to_all(jnp.stack([keyval] * lax.axis_size("seq")), "seq", 0, 0), axis=0
+    )
     piece_rows = incoming_keys.shape[0]
     step_rows = 512
 

time: 261 us -> 242 us (0.927)
  between operations: 14.4 us -> 1.05 us
  waiting for transfers between devices: 75.1 us -> 64.1 us
  starting transfers between devices: 18.6 us -> 26.8 us
    all_gather x1 -> x0, waiting for transfers between devices: 22.6 us -> none  [on_device(): incoming_keys = lax.all_gather(keyval, 'seq', axis=0, tiled=True)]
    all_to_all x0 -> x1, waiting for transfers between devices: none -> 11.5 us  [on_device(): lax.all_to_all(jnp.stack([keyval] * lax.axis_size('seq')), 'seq', 0, 0)]
    all_to_all x0 -> x1, starting transfers between devices: none -> 8.26 us  [on_device(): lax.all_to_all(jnp.stack([keyval] * lax.axis_size('seq')), 'seq', 0, 0)]
    while x1 -> x0, local copies, waits for them, and re-layouts: 4.09 us -> none  [on_device(): finals = lax.fori_loop(0, piece_rows // step_rows, one_step, initial)]
where the time goes in v1:
time: 242 us; the launch traced here: 241 us
  matrix products  74.8 us (31%)
  waiting for transfers between devices  64.1 us (26%)
  local copies, waits for them, and re-layouts  47.8 us (20%)
  starting transfers between devices  26.8 us (11%)
  other arithmetic  20 us (8%)
  loops' own time  5.92 us (2%)
    all_to_all x1, waiting for transfers between devices, on_device(): lax.all_to_all(wide_rows, ('seq', 'vis'), split_axis=0, concat_axis=0, ti...  48.9 us
    dot_general x8, matrix products, attend_block(): jnp.einsum('qgjd,kgd->qgjk', grouped, key_part, preferred_element_type=jn...  30.6 us
    dot_general x8, matrix products, attend_block(): jnp.einsum('qgjk,kgd->qgjd', raised.astype(jnp.bfloat16), value_part, pre...  28.5 us
    dot_general x1, matrix products, on_device(): jnp.dot(normed, w_query, preferred_element_type=jnp.float32) + q_bias  12.3 us
    gather x1, local copies, waits for them, and re-layouts, place_frames(): return jnp.where(covered[:, None], incoming[source], text)  11.7 us
    all_to_all x1, waiting for transfers between devices, on_device(): lax.all_to_all(jnp.stack([keyval] * lax.axis_size('seq')), 'seq', 0, 0)  11.5 us
    all_to_all x1, starting transfers between devices, on_device(): lax.all_to_all(wide_place, ('seq', 'vis'), split_axis=0, concat_axis=0, t...  10.4 us
    all_to_all x1, starting transfers between devices, on_device(): lax.all_to_all(jnp.stack([keyval] * lax.axis_size('seq')), 'seq', 0, 0)  8.26 us
  transfers between devices with their start and end apart: 3, of which 3 were waited for; matrix products, arithmetic and copies ran while one was open for 7% of the time, Pallas kernels for 0%

profile of v1, /device:TPU:57, one launch (start us, length us, event | category | flops | bytes accessed | tf_op | source)
XLA Modules:
  0.0 240.5 jit_solution(12456207047063107826)
XLA Ops:
  4.7 10.4 %all-to-all-start = ((s32[128,1,2]{2,1,0:T(1,128)}), s32[128,1,2]{2,1,0:T(1,128)S(1)}, u32[]{:S(2)}, u32[]{:S(2)}) async-start(s32[128,1,2]{2,1,0:T(1,128)} %bitcast.16), calls=%async_computation | async-start | bytes 131072 | tf_op jit(solution)/shard_map/all_to_all | solution.py:91
  22.1 6.1 %broadcast_in_dim.133 = bf16[16,8,2,8192]{3,2,1,0:T(2,128)(2,1)} broadcast(bf16[16,2,8192]{2,1,0:T(2,128)(2,1)S(1)} %broadcast_select_fusion.1), dimensions={0,2,3} | broadcast | bytes 4718592 | tf_op jit(solution)/shard_map/broadcast_in_dim | solution.py:85
  28.3 8.2 %all-to-all-start.1 = ((bf16[128,2,8192]{2,1,0:T(2,128)(2,1)}), bf16[128,2,8192]{2,1,0:T(2,128)(2,1)}, u32[]{:S(2)}, u32[]{:S(2)}) async-start(bf16[128,2,8192]{2,1,0:T(2,128)(2,1)} %bitcast.84), calls=%async_computation.1 | async-start | bytes 8388608 | tf_op jit(solution)/shard_map/all_to_all | solution.py:90
  37.1 48.9 %all-to-all-done.1 = bf16[128,2,8192]{2,1,0:T(2,128)(2,1)} async-done(((bf16[128,2,8192]{2,1,0:T(2,128)(2,1)}), bf16[128,2,8192]{2,1,0:T(2,128)(2,1)}, u32[]{:S(2)}, u32[]{:S(2)}) %all-to-all-start.1) | async-done | bytes 4194336 | tf_op jit(solution)/shard_map/all_to_all | solution.py:90
  86.0 7.2 %reshape.196 = bf16[256,8192]{1,0:T(8,128)(2,1)} reshape(bf16[128,2,8192]{2,1,0:T(2,128)(2,1)} %all-to-all-done.1) | data formatting | bytes 8388608 | tf_op jit(solution)/shard_map/reshape | solution.py:93
  93.2 11.7 %gather_fusion.2 = bf16[256,8192]{1,0:T(8,128)(2,1)} fusion(bf16[256,8192]{1,0:T(8,128)(2,1)} %reshape.196, s32[1024]{0:T(1024)S(1)} %pad_clamp_fusion), kind=kCustom, calls=%fused_computation.2 | custom fusion | bytes 8389632 | tf_op jit(solution)/shard_map/gather | solution.py:40
  104.8 5.1 %fusion.22 = f32[256]{0:T(256)S(1)} fusion(bf16[256,8192]{1,0:T(8,128)(2,1)} %gather_fusion.2, bf16[256,8192]{1,0:T(8,128)(2,1)} %param.15, pred[256]{0:T(512)(128)(4,1)S(1)} %fusion.28), kind=kLoop, calls=%fused_computation.31 | loop fusion | flops 8388352 | bytes 8389888 | tf_op jit(solution)/shard_map/reduce_sum | solution.py:97
  119.9 8.3 %all-to-all-start.2 = ((bf16[16,256,256]{2,1,0:T(8,128)(2,1)}), bf16[16,256,256]{2,1,0:T(8,128)(2,1)}, u32[]{:S(2)}, u32[]{:S(2)}) async-start(bf16[16,256,256]{2,1,0:T(8,128)(2,1)} %stack.2), calls=%async_computation.2 | async-start | bytes 4194304 | tf_op jit(solution)/shard_map/all_to_all | solution.py:123
  128.9 12.3 %fusion.25 = bf16[256,1024]{1,0:T(8,128)(2,1)} fusion(bf16[256,8192]{1,0:T(8,128)(2,1)} %copy-done.2, bf16[8192,1024]{1,0:T(8,128)(2,1)} %param.21, f32[1024]{0:T(1024)S(1)} %copy-done.8), kind=kOutput, calls=%fused_computation.36 | convolution fusion | flops 4295491584 | bytes 21499904 | tf_op jit(solution)/shard_map/dot_general | solution.py:99
  141.2 11.5 %all-to-all-done.2 = bf16[16,256,256]{2,1,0:T(8,128)(2,1)} async-done(((bf16[16,256,256]{2,1,0:T(8,128)(2,1)}), bf16[16,256,256]{2,1,0:T(8,128)(2,1)}, u32[]{:S(2)}, u32[]{:S(2)}) %all-to-all-start.2) | async-done | bytes 2097184 | tf_op jit(solution)/shard_map/all_to_all | solution.py:123
  152.9 84.8 %while.17 = (s32[]{:T(128)}, f32[256,1,8]{0,2,1:T(8,128)S(1)}, f32[256,1,8]{0,2,1:T(8,128)S(1)}, f32[256,1,8,128]{0,3,2,1:T(8,128)S(1)}, s32[256]{0:T(256)S(1)},...) while((s32[]{:T(128)}, f32[256,1,8]{0,2,1:T(8,128)S(1)}, ...), condition=%wide.region_11.12_spmd, body=%wide.region_6.11_spmd.sunk | while | flops 549329408 | bytes 32915828 | solution.py:157
  154.1 9.3 %conditional.2 = ((f32[256,1,8]{0,2,1:T(8,128)S(1)}, f32[256,1,8]{0,2,1:T(8,128)S(1)}, f32[256,1,8,128]{0,3,2,1:T(8,128)S(1)})) conditional(s32[]{:T(128)} %convert_element_type.65, (f32[256,1,8]{0,2,1:T(8,128)S(1)}, f32[256,1,8]{0,2,1:T(8,128)S(1)}, f32[256,1,8,128]{0,3,2,1:T(8,128)S(1)}) %tuple.48, (s32[]{:T(128)}, s32[512]{0:T(512)S(1)}, ...), branch_computations={%region_7.7_spmd, %region_8.10_spmd} | conditional | flops 549329408 | bytes 32913534 | solution.py:154
  155.1 3.8 %fusion = (f32[256,8]{0,1:T(8,128)S(1)}, f32[512,256,8]{1,0,2:T(8,128)}) fusion(pred[256,512]{0,1:T(8,128)(4,1)S(1)} %compare_and_fusion, bf16[4096,256]{1,0:T(8,128)(2,1)} %get-tuple-element.272, s32[]{:T(128)S(6)} %select_n.70, bf16[256,1024]{1,0:T(8,128)(2,1)} %get-tuple-element.273), kind=kOutput, calls=%fused_computation.5 | convolution fusion | flops 271579136 | bytes 4988932 | tf_op jit(solution)/shard_map/while/body/eval_jaxpr/cond/branch_1_fun/qgjd,kgd->qgjk/dot_general | solution.py:52
  164.7 9.3 %conditional.2 = ((f32[256,1,8]{0,2,1:T(8,128)S(1)}, f32[256,1,8]{0,2,1:T(8,128)S(1)}, f32[256,1,8,128]{0,3,2,1:T(8,128)S(1)})) conditional(s32[]{:T(128)} %convert_element_type.65, (f32[256,1,8]{0,2,1:T(8,128)S(1)}, f32[256,1,8]{0,2,1:T(8,128)S(1)}, f32[256,1,8,128]{0,3,2,1:T(8,128)S(1)}) %tuple.48, (s32[]{:T(128)}, s32[512]{0:T(512)S(1)}, ...), branch_computations={%region_7.7_spmd, %region_8.10_spmd} | conditional | flops 549329408 | bytes 32913534 | solution.py:154
  165.7 3.8 %fusion = (f32[256,8]{0,1:T(8,128)S(1)}, f32[512,256,8]{1,0,2:T(8,128)}) fusion(pred[256,512]{0,1:T(8,128)(4,1)S(1)} %compare_and_fusion, bf16[4096,256]{1,0:T(8,128)(2,1)} %get-tuple-element.272, s32[]{:T(128)S(6)} %select_n.70, bf16[256,1024]{1,0:T(8,128)(2,1)} %get-tuple-element.273), kind=kOutput, calls=%fused_computation.5 | convolution fusion | flops 271579136 | bytes 4988932 | tf_op jit(solution)/shard_map/while/body/eval_jaxpr/cond/branch_1_fun/qgjd,kgd->qgjk/dot_general | solution.py:52
  175.3 9.3 %conditional.2 = ((f32[256,1,8]{0,2,1:T(8,128)S(1)}, f32[256,1,8]{0,2,1:T(8,128)S(1)}, f32[256,1,8,128]{0,3,2,1:T(8,128)S(1)})) conditional(s32[]{:T(128)} %convert_element_type.65, (f32[256,1,8]{0,2,1:T(8,128)S(1)}, f32[256,1,8]{0,2,1:T(8,128)S(1)}, f32[256,1,8,128]{0,3,2,1:T(8,128)S(1)}) %tuple.48, (s32[]{:T(128)}, s32[512]{0:T(512)S(1)}, ...), branch_computations={%region_7.7_spmd, %region_8.10_spmd} | conditional | flops 549329408 | bytes 32913534 | solution.py:154
  176.3 3.8 %fusion = (f32[256,8]{0,1:T(8,128)S(1)}, f32[512,256,8]{1,0,2:T(8,128)}) fusion(pred[256,512]{0,1:T(8,128)(4,1)S(1)} %compare_and_fusion, bf16[4096,256]{1,0:T(8,128)(2,1)} %get-tuple-element.272, s32[]{:T(128)S(6)} %select_n.70, bf16[256,1024]{1,0:T(8,128)(2,1)} %get-tuple-element.273), kind=kOutput, calls=%fused_computation.5 | convolution fusion | flops 271579136 | bytes 4988932 | tf_op jit(solution)/shard_map/while/body/eval_jaxpr/cond/branch_1_fun/qgjd,kgd->qgjk/dot_general | solution.py:52
  185.9 9.3 %conditional.2 = ((f32[256,1,8]{0,2,1:T(8,128)S(1)}, f32[256,1,8]{0,2,1:T(8,128)S(1)}, f32[256,1,8,128]{0,3,2,1:T(8,128)S(1)})) conditional(s32[]{:T(128)} %convert_element_type.65, (f32[256,1,8]{0,2,1:T(8,128)S(1)}, f32[256,1,8]{0,2,1:T(8,128)S(1)}, f32[256,1,8,128]{0,3,2,1:T(8,128)S(1)}) %tuple.48, (s32[]{:T(128)}, s32[512]{0:T(512)S(1)}, ...), branch_computations={%region_7.7_spmd, %region_8.10_spmd} | conditional | flops 549329408 | bytes 32913534 | solution.py:154
  186.9 3.8 %fusion = (f32[256,8]{0,1:T(8,128)S(1)}, f32[512,256,8]{1,0,2:T(8,128)}) fusion(pred[256,512]{0,1:T(8,128)(4,1)S(1)} %compare_and_fusion, bf16[4096,256]{1,0:T(8,128)(2,1)} %get-tuple-element.272, s32[]{:T(128)S(6)} %select_n.70, bf16[256,1024]{1,0:T(8,128)(2,1)} %get-tuple-element.273), kind=kOutput, calls=%fused_computation.5 | convolution fusion | flops 271579136 | bytes 4988932 | tf_op jit(solution)/shard_map/while/body/eval_jaxpr/cond/branch_1_fun/qgjd,kgd->qgjk/dot_general | solution.py:52
  196.5 9.3 %conditional.2 = ((f32[256,1,8]{0,2,1:T(8,128)S(1)}, f32[256,1,8]{0,2,1:T(8,128)S(1)}, f32[256,1,8,128]{0,3,2,1:T(8,128)S(1)})) conditional(s32[]{:T(128)} %convert_element_type.65, (f32[256,1,8]{0,2,1:T(8,128)S(1)}, f32[256,1,8]{0,2,1:T(8,128)S(1)}, f32[256,1,8,128]{0,3,2,1:T(8,128)S(1)}) %tuple.48, (s32[]{:T(128)}, s32[512]{0:T(512)S(1)}, ...), branch_computations={%region_7.7_spmd, %region_8.10_spmd} | conditional | flops 549329408 | bytes 32913534 | solution.py:154
  197.5 3.8 %fusion = (f32[256,8]{0,1:T(8,128)S(1)}, f32[512,256,8]{1,0,2:T(8,128)}) fusion(pred[256,512]{0,1:T(8,128)(4,1)S(1)} %compare_and_fusion, bf16[4096,256]{1,0:T(8,128)(2,1)} %get-tuple-element.272, s32[]{:T(128)S(6)} %select_n.70, bf16[256,1024]{1,0:T(8,128)(2,1)} %get-tuple-element.273), kind=kOutput, calls=%fused_computation.5 | convolution fusion | flops 271579136 | bytes 4988932 | tf_op jit(solution)/shard_map/while/body/eval_jaxpr/cond/branch_1_fun/qgjd,kgd->qgjk/dot_general | solution.py:52
  207.1 9.3 %conditional.2 = ((f32[256,1,8]{0,2,1:T(8,128)S(1)}, f32[256,1,8]{0,2,1:T(8,128)S(1)}, f32[256,1,8,128]{0,3,2,1:T(8,128)S(1)})) conditional(s32[]{:T(128)} %convert_element_type.65, (f32[256,1,8]{0,2,1:T(8,128)S(1)}, f32[256,1,8]{0,2,1:T(8,128)S(1)}, f32[256,1,8,128]{0,3,2,1:T(8,128)S(1)}) %tuple.48, (s32[]{:T(128)}, s32[512]{0:T(512)S(1)}, ...), branch_computations={%region_7.7_spmd, %region_8.10_spmd} | conditional | flops 549329408 | bytes 32913534 | solution.py:154
  217.7 9.3 %conditional.2 = ((f32[256,1,8]{0,2,1:T(8,128)S(1)}, f32[256,1,8]{0,2,1:T(8,128)S(1)}, f32[256,1,8,128]{0,3,2,1:T(8,128)S(1)})) conditional(s32[]{:T(128)} %convert_element_type.65, (f32[256,1,8]{0,2,1:T(8,128)S(1)}, f32[256,1,8]{0,2,1:T(8,128)S(1)}, f32[256,1,8,128]{0,3,2,1:T(8,128)S(1)}) %tuple.48, (s32[]{:T(128)}, s32[512]{0:T(512)S(1)}, ...), branch_computations={%region_7.7_spmd, %region_8.10_spmd} | conditional | flops 549329408 | bytes 32913534 | solution.py:154
  228.3 9.3 %conditional.2 = ((f32[256,1,8]{0,2,1:T(8,128)S(1)}, f32[256,1,8]{0,2,1:T(8,128)S(1)}, f32[256,1,8,128]{0,3,2,1:T(8,128)S(1)})) conditional(s32[]{:T(128)} %convert_element_type.65, (f32[256,1,8]{0,2,1:T(8,128)S(1)}, f32[256,1,8]{0,2,1:T(8,128)S(1)}, f32[256,1,8,128]{0,3,2,1:T(8,128)S(1)}) %tuple.48, (s32[]{:T(128)}, s32[512]{0:T(512)S(1)}, ...), branch_computations={%region_7.7_spmd, %region_8.10_spmd} | conditional | flops 549329408 | bytes 32913534 | solution.py:154
  (152 shorter events, 84.8 us)
Async XLA Ops:
  0.0 113.5 %copy-start = (bf16[8192,128]{1,0:T(8,128)(2,1)S(1)}, bf16[8192,128]{1,0:T(8,128)(2,1)}, u32[]{:S(2)}) copy-start(bf16[8192,128]{1,0:T(8,128)(2,1)} %param.23) | copy-start | bytes 6291460
  4.7 17.4 %all-to-all-start = ((s32[128,1,2]{2,1,0:T(1,128)}), s32[128,1,2]{2,1,0:T(1,128)S(1)}, u32[]{:S(2)}, u32[]{:S(2)}) async-start(s32[128,1,2]{2,1,0:T(1,128)} %bitcast.16), calls=%async_computation | async-start | bytes 131072 | tf_op jit(solution)/shard_map/all_to_all | solution.py:91
  28.3 57.7 %all-to-all-start.1 = ((bf16[128,2,8192]{2,1,0:T(2,128)(2,1)}), bf16[128,2,8192]{2,1,0:T(2,128)(2,1)}, u32[]{:S(2)}, u32[]{:S(2)}) async-start(bf16[128,2,8192]{2,1,0:T(2,128)(2,1)} %bitcast.84), calls=%async_computation.1 | async-start | bytes 8388608 | tf_op jit(solution)/shard_map/all_to_all | solution.py:90
  93.2 16.8 %copy-start.6 = (f32[8192]{0:T(1024)S(1)}, f32[8192]{0:T(1024)}, u32[]{:S(2)}) copy-start(f32[8192]{0:T(1024)} %param.20) | copy-start | bytes 98308
  104.8 5.2 %copy-start.3 = (bf16[256,8192]{1,0:T(8,128)(2,1)S(1)}, bf16[256,8192]{1,0:T(8,128)(2,1)}, u32[]{:S(2)}) copy-start(bf16[256,8192]{1,0:T(8,128)(2,1)} %gather_fusion.2) | copy-start | bytes 12582916
  104.8 5.9 %copy-start.4 = (bf16[256,8192]{1,0:T(8,128)(2,1)S(1)}, bf16[256,8192]{1,0:T(8,128)(2,1)}, u32[]{:S(2)}) copy-start(bf16[256,8192]{1,0:T(8,128)(2,1)} %param.15) | copy-start | bytes 12582916
  113.5 4.7 %copy-start.2 = (bf16[256,8192]{1,0:T(8,128)(2,1)}, bf16[256,8192]{1,0:T(8,128)(2,1)S(1)}, u32[]{:S(2)}) copy-start(bf16[256,8192]{1,0:T(8,128)(2,1)S(1)} %fusion.24) | copy-start | bytes 12582916
  113.5 3.1 %copy-start.5 = (bf16[8192,128]{1,0:T(8,128)(2,1)S(1)}, bf16[8192,128]{1,0:T(8,128)(2,1)}, u32[]{:S(2)}) copy-start(bf16[8192,128]{1,0:T(8,128)(2,1)} %param.24) | copy-start | bytes 6291460
  113.5 3.1 %copy-start.7 = (f32[128]{0:T(128)S(1)}, f32[128]{0:T(128)}, u32[]{:S(2)}) copy-start(f32[128]{0:T(128)} %param.25) | copy-start | bytes 1540
  118.2 10.7 %copy-start.8 = (f32[1024]{0:T(1024)S(1)}, f32[1024]{0:T(1024)}, u32[]{:S(2)}) copy-start(f32[1024]{0:T(1024)} %param.22) | copy-start | bytes 12292
  119.9 32.9 %all-to-all-start.2 = ((bf16[16,256,256]{2,1,0:T(8,128)(2,1)}), bf16[16,256,256]{2,1,0:T(8,128)(2,1)}, u32[]{:S(2)}, u32[]{:S(2)}) async-start(bf16[16,256,256]{2,1,0:T(8,128)(2,1)} %stack.2), calls=%async_computation.2 | async-start | bytes 4194304 | tf_op jit(solution)/shard_map/all_to_all | solution.py:123
  159.0 3.6 %copy-start.1 = (f32[512,256,8]{1,0,2:T(8,128)S(1)}, f32[512,256,8]{1,0,2:T(8,128)}, u32[]{:S(2)}) copy-start(f32[512,256,8]{1,0,2:T(8,128)} %get-tuple-element.314) | copy-start | bytes 12582916 | tf_op jit(solution)/shard_map/while/body/eval_jaxpr/cond
  169.6 3.6 %copy-start.1 = (f32[512,256,8]{1,0,2:T(8,128)S(1)}, f32[512,256,8]{1,0,2:T(8,128)}, u32[]{:S(2)}) copy-start(f32[512,256,8]{1,0,2:T(8,128)} %get-tuple-element.314) | copy-start | bytes 12582916 | tf_op jit(solution)/shard_map/while/body/eval_jaxpr/cond
  180.2 3.6 %copy-start.1 = (f32[512,256,8]{1,0,2:T(8,128)S(1)}, f32[512,256,8]{1,0,2:T(8,128)}, u32[]{:S(2)}) copy-start(f32[512,256,8]{1,0,2:T(8,128)} %get-tuple-element.314) | copy-start | bytes 12582916 | tf_op jit(solution)/shard_map/while/body/eval_jaxpr/cond
  190.8 3.6 %copy-start.1 = (f32[512,256,8]{1,0,2:T(8,128)S(1)}, f32[512,256,8]{1,0,2:T(8,128)}, u32[]{:S(2)}) copy-start(f32[512,256,8]{1,0,2:T(8,128)} %get-tuple-element.314) | copy-start | bytes 12582916 | tf_op jit(solution)/shard_map/while/body/eval_jaxpr/cond
  201.4 3.6 %copy-start.1 = (f32[512,256,8]{1,0,2:T(8,128)S(1)}, f32[512,256,8]{1,0,2:T(8,128)}, u32[]{:S(2)}) copy-start(f32[512,256,8]{1,0,2:T(8,128)} %get-tuple-element.314) | copy-start | bytes 12582916 | tf_op jit(solution)/shard_map/while/body/eval_jaxpr/cond
  211.9 3.6 %copy-start.1 = (f32[512,256,8]{1,0,2:T(8,128)S(1)}, f32[512,256,8]{1,0,2:T(8,128)}, u32[]{:S(2)}) copy-start(f32[512,256,8]{1,0,2:T(8,128)} %get-tuple-element.314) | copy-start | bytes 12582916 | tf_op jit(solution)/shard_map/while/body/eval_jaxpr/cond
  222.5 3.6 %copy-start.1 = (f32[512,256,8]{1,0,2:T(8,128)S(1)}, f32[512,256,8]{1,0,2:T(8,128)}, u32[]{:S(2)}) copy-start(f32[512,256,8]{1,0,2:T(8,128)} %get-tuple-element.314) | copy-start | bytes 12582916 | tf_op jit(solution)/shard_map/while/body/eval_jaxpr/cond
  233.1 3.6 %copy-start.1 = (f32[512,256,8]{1,0,2:T(8,128)S(1)}, f32[512,256,8]{1,0,2:T(8,128)}, u32[]{:S(2)}) copy-start(f32[512,256,8]{1,0,2:T(8,128)} %get-tuple-element.314) | copy-start | bytes 12582916 | tf_op jit(solution)/shard_map/while/body/eval_jaxpr/cond
